TPU v7x, 32 devices: a whole 2x2x4 slice. The times are simulated.
32 devices in a mesh: groups: 2 (over y), seq: 4 (over z), head: 2 (over x), sub: 2 (over core).
Axes of the slice: x: 2, y: 2, z: 4, core: 2. Of those that a mesh axis runs over, the one named last changes fastest.
Arguments:
- x_raw: bfloat16 [16, 128, 8192], P(('groups', 'seq', 'sub'), 'head'), parts along dimension 0, may hold values from -6 to 6
- bc_raw: bfloat16 [16, 128, 2048], P(('groups', 'seq', 'sub'), 'head'), parts along dimension 0, may hold values from -6 to 6
- dt_raw: bfloat16 [16, 128, 128], P(('groups', 'seq', 'sub'), 'head'), parts along dimension 0, may hold values from -3 to 40
- conv_x_weight: float32 [4, 8192], P(None, 'head'), may hold values from -3 to 3
- conv_x_bias: float32 [8192], P('head'), may hold values from -2.5 to 2.5
- conv_bc_weight: float32 [4, 2048], P(None, 'head'), may hold values from -3 to 3
- conv_bc_bias: float32 [2048], P('head'), may hold values from -2.5 to 2.5
- stride_offset_per_head: float32 [128], P('head'), may hold values from -12 to 0
- a_log: float32 [128], P('head'), may hold values from -8 to 3
- skip_d: float32 [128], P('head'), may hold values from 0.5 to 1.5
- norm_gain: float32 [8192], P('head'), may hold values from 0.1 to 1.9
Outputs:
- mixed: bfloat16 [16, 128, 8192], P(('groups', 'seq', 'sub'), None, 'head'), parts along dimension 0
There are 2 independent parts, one for each index of `groups`. A program takes and returns all parts, laid end to end along the dimension named above; an argument that names none is the same for every part. Nothing has to cross between parts.
All inputs are finite; a program needn't handle non-finite values.
Results may differ from a plain program's by a relative error of at most 0.0061.
Values may be sent and summed in bfloat16 or wider, within the bound.
No kernel may reach another device: no remote copies, remote signals or barrier semaphores. Data moves between devices by JAX's collectives and lax.ppermute only.
A program may use at most 128 MiB of HBM per device.

v0:
```python
import jax
import jax.numpy as jnp
from jax import lax
from jax.sharding import PartitionSpec as P

STATE = 128
SPAN = 128
NORM_EPSILON = 1e-05


def shifted(value, axis, steps):
    count = lax.axis_size(axis)
    leading, last = (max(0, -steps), min(count, count - steps))
    return lax.ppermute(value, axis, [(source, source + steps) for source in range(leading, last)])


def from_partner(shard, axis, distance):
    return lax.ppermute(shard, axis, [(i, i ^ 1 << distance) for i in range(lax.axis_size(axis))])


def prefix_2(shard, axis, combine, identity):
    length, position = (lax.axis_size(axis), lax.axis_index(axis))
    everything = jax.tree.map(lambda part: lax.all_gather(part, axis), shard)
    start = jax.tree.map(
        lambda part, zero: jnp.broadcast_to(jnp.asarray(zero, part.dtype), part.shape),
        shard,
        identity,
    )

    def hop(k, before):
        reached = k < position
        new = combine(before, jax.tree.map(lambda part: part[k], everything))
        return jax.tree.map(lambda a, b: jnp.where(reached, a, b), new, before)

    return lax.fori_loop(0, length, hop, start)


def conv_rows(raw_rows, rim_rows, weight, bias):
    conv_width = weight.shape[0]
    row_count = raw_rows.shape[0]
    joined = jnp.concatenate([rim_rows, raw_rows], axis=0).astype(jnp.float32)
    running = bias[None, :]
    for tap_index in range(conv_width):
        running = running + weight[tap_index][None, :] * joined[tap_index : tap_index + row_count]
    return jax.nn.silu(running).astype(jnp.bfloat16)


def chain_step(earlier, later_part):
    decay_early, state_early = earlier
    decay_later, state_later = later_part
    return (decay_early * decay_later, decay_later[..., None] * state_early + state_later)


def on_device(
    x_raw,
    bc_raw,
    dt_raw,
    conv_x_weight,
    conv_x_bias,
    conv_bc_weight,
    conv_bc_bias,
    stride_offset_per_head,
    a_log,
    skip_d,
    norm_gain,
):
    x_ex, bc_ex, dt_ex = (
        lax.all_to_all(x_raw, "head", split_axis=2, concat_axis=1, tiled=True),
        lax.all_to_all(bc_raw, "head", split_axis=2, concat_axis=1, tiled=True),
        lax.all_to_all(dt_raw, "head", split_axis=2, concat_axis=1, tiled=True),
    )
    x_rows = x_ex[0]
    bc_rows = bc_ex[0]
    dt_rows = dt_ex[0]
    conv_width = conv_x_weight.shape[0]
    x_rim, bc_rim = shifted(
        (x_rows[x_rows.shape[0] - conv_width + 1 :], bc_rows[bc_rows.shape[0] - conv_width + 1 :]),
        ("seq", "sub"),
        1,
    )
    x_conv = conv_rows(x_rows, x_rim, conv_x_weight, conv_x_bias)
    bc_conv = conv_rows(bc_rows, bc_rim, conv_bc_weight, conv_bc_bias)
    row_count = x_conv.shape[0]
    head_count = dt_rows.shape[1]
    groups = bc_conv.shape[1] // (2 * STATE)
    per_group = head_count // groups
    head_dim = x_conv.shape[1] // head_count
    group_width = per_group * head_dim
    span_len = SPAN
    blocks = row_count // span_len
    dt_step = jax.nn.softplus(dt_rows.astype(jnp.float32) + stride_offset_per_head[None, :])
    decay_rate = -jnp.exp(a_log)
    decay_logarithm_rows = (decay_rate[None, :] * dt_step).reshape(blocks, span_len, head_count)
    cum_decay = jnp.cumsum(decay_logarithm_rows, axis=1)
    step_blocks = dt_step.reshape(blocks, span_len, head_count)
    x_blocks = x_conv.reshape(blocks, span_len, groups, per_group, head_dim)
    x_wide = x_conv.reshape(blocks, span_len, groups, group_width)
    bc_blocks = bc_conv.reshape(blocks, span_len, groups, 2, STATE)
    b_in = bc_blocks[:, :, :, 0]
    c_out = bc_blocks[:, :, :, 1]

    def widen(per_head):
        return jnp.repeat(per_head, head_dim, axis=-1).reshape(
            per_head.shape[:-1] + (groups, group_width)
        )

    causal = lax.broadcasted_iota(jnp.int32, (span_len, span_len), 0) >= lax.broadcasted_iota(
        jnp.int32, (span_len, span_len), 1
    )
    inner_prod = jnp.einsum("btgn,bsgn->bgts", c_out, b_in, preferred_element_type=jnp.float32)
    cum_heads = jnp.transpose(cum_decay, (0, 2, 1)).reshape(blocks, groups, per_group, span_len)
    step_heads = jnp.transpose(step_blocks, (0, 2, 1)).reshape(blocks, groups, per_group, span_len)
    gap_pairs = cum_heads[..., :, None] - cum_heads[..., None, :]
    weight = jnp.exp(jnp.where(causal, gap_pairs, -1e30)) * step_heads[..., None, :]
    mixing = (inner_prod[:, :, None] * weight).astype(jnp.bfloat16)
    within_block_output = jnp.einsum(
        "bgjts,bsgjp->btgjp", mixing, x_blocks, preferred_element_type=jnp.float32
    )
    within_wide = within_block_output.reshape(blocks, span_len, groups, group_width)
    block_end = cum_decay[:, span_len - 1 :, :]
    to_end = jnp.exp(block_end - cum_decay) * step_blocks
    scaled = (widen(to_end) * x_wide).astype(jnp.bfloat16)
    states = jnp.einsum("bsgq,bsgn->bgqn", scaled, b_in, preferred_element_type=jnp.float32)
    decays = widen(jnp.exp(block_end[:, 0, :]))
    identity = (
        jnp.ones((groups, group_width), jnp.float32),
        jnp.zeros((groups, group_width, STATE), jnp.float32),
    )

    def local_step(running, block_item):
        return (chain_step(running, block_item), running)

    own_part, prefix = lax.scan(local_step, identity, (decays, states))
    partner = from_partner((own_part[0], own_part[1]), "sub", 0)
    is_lower = lax.axis_index("sub") == 0
    first_part = jax.tree.map(
        lambda mine, other: jnp.where(is_lower, mine, other), own_part, partner
    )
    second_part = jax.tree.map(
        lambda mine, other: jnp.where(is_lower, other, mine), own_part, partner
    )
    pair_total = chain_step(first_part, second_part)
    before_pair = prefix_2(pair_total, "seq", chain_step, identity)
    inside_pair = jax.tree.map(
        lambda empty, other: jnp.where(is_lower, empty, other), identity, partner
    )
    entry_part = chain_step(before_pair, inside_pair)
    device_entry = entry_part[1]
    carried = prefix[0][..., None] * device_entry[None] + prefix[1]
    carried_bf = carried.astype(jnp.bfloat16)
    y_state = jnp.einsum("btgn,bgqn->btgq", c_out, carried_bf, preferred_element_type=jnp.float32)
    y_state = y_state * widen(jnp.exp(cum_decay))
    skip_wide = jnp.repeat(skip_d, head_dim).reshape(groups, group_width)
    complete_output = within_wide + y_state + skip_wide * x_wide
    squares_mean = jnp.mean(complete_output * complete_output, axis=3)
    normed = (
        complete_output
        * lax.rsqrt(squares_mean + NORM_EPSILON)[..., None]
        * norm_gain.reshape(groups, group_width)
    )
    return normed.reshape(row_count, head_count * head_dim).astype(jnp.bfloat16)[None]


def solution(mesh):
    placed = (
        P(("groups", "seq", "sub"), "head", None),
        P(("groups", "seq", "sub"), "head", None),
        P(("groups", "seq", "sub"), "head", None),
        P(None, "head"),
        P("head"),
        P(None, "head"),
        P("head"),
        P("head"),
        P("head"),
        P("head"),
        P("head"),
    )
    return jax.shard_map(
        on_device,
        mesh=mesh,
        in_specs=placed,
        out_specs=P(("groups", "seq", "sub"), None, "head"),
        check_vma=False,
    )
```

profile of v0, /device:TPU:0, one launch (start us, length us, event | category | flops | bytes accessed | tf_op | source)
XLA Modules:
  0.0 315.5 jit_solution(2477985931013234938)
XLA Ops:
  6.5 0.8 copy.58
  7.4 0.6 broadcast.182
  8.0 0.9 reduce.6
  8.8 0.7 reshape.322
  9.6 4.2 %all-to-all-start.2 = ((bf16[2,2,2048]{2,1,0:T(2,128)(2,1)}), bf16[2,2,2048]{2,1,0:T(2,128)(2,1)S(1)}, u32[]{:S(2)}, u32[]{:S(2)}) async-start(bf16[2,2,2048]{2,1,0:T(2,128)(2,1)} %reshape.322), calls=%async_computation.2 | async-start | bytes 32768 | tf_op jit(solution)/shard_map/all_to_all | solution.py:70
  13.8 1.7 fusion.27
  15.5 0.9 fusion.28
  16.3 0.7 exponential_negate_fusion
  17.0 9.2 %copy.48 = bf16[1,64,8192]{1,0,2:T(2,128)(2,1)} copy(bf16[1,64,8192]{2,1,0:T(8,128)(2,1)} %param.13) | data formatting | bytes 2097152 | tf_op args[0]
  26.2 45.3 %reduce.5 = bf16[8192,64]{1,0:T(8,128)(2,1)S(1)} reduce(bf16[8192,1,64]{2,1,0:T(2,128)(2,1)} %bitcast.99, bf16[]{:T(256)} %broadcast.182), dimensions={1}, to_apply=%bitcast.80.reduce_sub_computation | reduce | bytes 2097154
  71.5 2.4 reshape.320
  73.9 0.7 copy.52
  74.6 11.8 %reduce.7 = bf16[2048,64]{1,0:T(8,128)(2,1)S(1)} reduce(bf16[2048,1,64]{2,1,0:T(2,128)(2,1)S(1)} %bitcast.106, bf16[]{:T(256)} %broadcast.182), dimensions={1}, to_apply=%bitcast.84.reduce_sub_computation | reduce | bytes 524290
  86.4 1.1 reshape.324
  87.5 3.4 %all-to-all-start.1 = ((bf16[2,2,32768]{2,1,0:T(2,128)(2,1)}), bf16[2,2,32768]{2,1,0:T(2,128)(2,1)S(1)}, u32[]{:S(2)}, u32[]{:S(2)}) async-start(bf16[2,2,32768]{2,1,0:T(2,128)(2,1)} %reshape.324), calls=%async_computation.1 | async-start | bytes 524288 | tf_op jit(solution)/shard_map/all_to_all | solution.py:69
  91.3 0.7 broadcast_multiply_fusion
  92.6 4.0 %all-to-all-done.1 = bf16[2,2,32768]{2,1,0:T(2,128)(2,1)S(1)} async-done(((bf16[2,2,32768]{2,1,0:T(2,128)(2,1)}), bf16[2,2,32768]{2,1,0:T(2,128)(2,1)S(1)}, u32[]{:S(2)}, u32[]{:S(2)}) %all-to-all-start.1) | async-done | bytes 262176 | tf_op jit(solution)/shard_map/all_to_all | solution.py:69
  96.6 3.6 %all-to-all-start = ((bf16[2,2,131072]{2,1,0:T(2,128)(2,1)}), bf16[2,2,131072]{2,1,0:T(2,128)(2,1)S(1)}, u32[]{:S(2)}, u32[]{:S(2)}) async-start(bf16[2,2,131072]{2,1,0:T(2,128)(2,1)} %reshape.320), calls=%async_computation | async-start | bytes 2097152 | tf_op jit(solution)/shard_map/all_to_all | solution.py:68
  100.3 0.7 copy.63
  101.0 0.4 reshape.325
  101.5 0.6 copy.53
  102.3 1.3 collective-permute-start.1
  103.7 0.6 broadcast_select_fusion.1
  104.5 8.9 %all-to-all-done = bf16[2,2,131072]{2,1,0:T(2,128)(2,1)S(1)} async-done(((bf16[2,2,131072]{2,1,0:T(2,128)(2,1)}), bf16[2,2,131072]{2,1,0:T(2,128)(2,1)S(1)}, u32[]{:S(2)}, u32[]{:S(2)}) %all-to-all-start) | async-done | bytes 1048608 | tf_op jit(solution)/shard_map/all_to_all | solution.py:68
  113.4 2.7 reshape.321
  116.2 8.2 %copy.49 = bf16[1,64,8192]{2,1,0:T(8,128)(2,1)S(1)} copy(bf16[1,64,8192]{1,0,2:T(2,128)(2,1)} %bitcast.98) | data formatting | bytes 2097152 | tf_op jit(solution)/shard_map/all_to_all | solution.py:68
  124.4 0.8 all_to_all.30
  125.2 0.6 copy.50
  125.8 1.3 collective-permute-start
  127.1 0.3 multiply_convert_fusion.4
  127.7 0.3 collective-permute-done
  127.9 0.3 maximum_convert_fusion
  128.3 1.3 multiply_convert_fusion.3
  129.6 0.5 copy.69
  130.2 0.9 broadcast_in_dim.66
  131.1 0.2 fusion.8
  131.3 0.2 copy-done
  131.6 0.3 copy-done.7
  131.8 0.7 convolution_add_fusion
  132.6 2.6 collective-permute-start.3
  135.1 3.8 %collective-permute-done.3 = f32[4,1024,128]{2,1,0:T(8,128)S(1)} collective-permute-done((f32[4,1024,128]{2,1,0:T(8,128)S(1)}, f32[4,1024,128]{2,1,0:T(8,128)S(1)}, u32[]{:S(2)}, u32[]{:S(2)}) %collective-permute-start.3) | collective-permute-done | bytes 2097184 | tf_op jit(solution)/shard_map/ppermute | solution.py:18
  138.9 1.3 copy-done.2
  140.3 1.7 select_add_fusion
  141.9 0.6 copy-done.17
  142.6 0.7 broadcast_in_dim.71
  143.3 0.8 broadcast_in_dim.72
  144.2 1.3 mul.290
  145.5 0.6 iota_compare_fusion
  146.1 0.7 copy.62
  146.8 0.7 copy.65
  147.5 15.4 %all-gather.2 = f32[4,4,1024]{2,1,0:T(4,128)S(1)} all-gather(f32[1,4,1024]{2,1,0:T(4,128)} %get-tuple-element.160), channel_id=2, replica_groups=mesh['groups'=2,'seq'=4,'head'=2,'sub'=2] {'seq'}, dimensions={0}, use_global_device_ids=true | all-gather | bytes 81920 | tf_op jit(solution)/shard_map/all_gather | solution.py:23
  162.9 0.9 fusion.22
  163.8 1.3 copy.51
  165.1 3.9 %fusion.1 = f32[4,16,64,128]{3,2,1,0:T(8,128)} fusion(bf16[128,4,16,64]{0,3,2,1:T(8,128)(2,1)} %bitcast.114, f32[4,16,128]{2,1,0:T(8,128)S(1)} %bitcast.124, f32[4,16,128]{2,1,0:T(8,128)S(1)} %bitcast.125, f32[4,128,128]{2,1,0:T(8,128)} %fusion.22, pred[128,128]{1,0:T(8,128)(4,1)} %iota_compare_fusion), kind=kOutput, calls=%fused_computation.4 | convolution fusion | flops 139460608 | bytes 3489792 | tf_op jit(solution)/shard_map/bgjts,bsgjp->btgjp/dot_general | solution.py:116
  169.0 124.5 %all-gather.5.cloned.1.call-done = f32[16,1024,128]{2,1,0:T(8,128)} async-done(((f32[4,1024,128]{2,1,0:T(8,128)}), f32[16,1024,128]{2,1,0:T(8,128)}) %all-gather.5.cloned.1.call-update) | async-done | bytes 8388624 | tf_op jit(solution)/shard_map/all_gather | solution.py:23
  293.5 8.8 %while.9 = (s32[]{:T(128)}, f32[4,1024,128]{2,1,0:T(8,128)S(1)}, s32[]{:T(128)}, f32[4,4,1024]{2,1,0:T(4,128)S(1)}, f32[4,4,1024,128]{3,2,1,0:T(8,128)}, /*index=5*/s32[]{:T(128)}, s32[]{:T(128)}) while((s32[]{:T(128)}, f32[4,1024,128]{2,1,0:T(8,128)S(1)}, s32[]{:T(128)}, f32[4,4,1024]{2,1,0:T(4,128)S(1)}, ...), condition=%wide.region_2.3_spmd.clone, body=%wide.region_1.2_spmd.clone.sunk | while | flops 2097156 | bytes 6340713 | solution.py:35
  293.5 2.2 fusion.32
  295.7 2.2 fusion.32
  297.9 2.2 fusion.32
  300.1 2.2 fusion.32
  302.5 1.4 copy-done.1
  303.9 2.6 multiply_reduce_fusion
  306.6 0.7 multiply_convert_fusion.2
  307.3 1.3 copy.67
  (62 shorter events, 2.0 us)
Async XLA Ops:
  9.6 78.0 %all-to-all-start.2 = ((bf16[2,2,2048]{2,1,0:T(2,128)(2,1)}), bf16[2,2,2048]{2,1,0:T(2,128)(2,1)S(1)}, u32[]{:S(2)}, u32[]{:S(2)}) async-start(bf16[2,2,2048]{2,1,0:T(2,128)(2,1)} %reshape.322), calls=%async_computation.2 | async-start | bytes 32768 | tf_op jit(solution)/shard_map/all_to_all | solution.py:70
  71.5 2.5 copy-start.3
  73.9 17.4 %copy-start.16 = (f32[64]{0:T(128)S(1)}, f32[64]{0:T(128)}, u32[]{:S(2)}) copy-start(f32[64]{0:T(128)} %param.20) | copy-start | bytes 772
  87.5 9.1 %all-to-all-start.1 = ((bf16[2,2,32768]{2,1,0:T(2,128)(2,1)}), bf16[2,2,32768]{2,1,0:T(2,128)(2,1)S(1)}, u32[]{:S(2)}, u32[]{:S(2)}) async-start(bf16[2,2,32768]{2,1,0:T(2,128)(2,1)} %reshape.324), calls=%async_computation.1 | async-start | bytes 524288 | tf_op jit(solution)/shard_map/all_to_all | solution.py:69
  92.6 11.1 %collective-permute-start.2 = (f32[4,1024]{1,0:T(4,128)S(1)}, f32[4,1024]{1,0:T(4,128)S(1)}, u32[]{:S(2)}, u32[]{:S(2)}) collective-permute-start(f32[4,1024]{1,0:T(4,128)S(1)} %broadcast_in_dim.63), channel_id=1, source_target_pairs={{0,1},{1,0},{2,3},{3,2},{4,5},{5,4},{6,7},{7,6},{8,9},{9,8},{10,11... | collective-permute-start | bytes 49160 | tf_op jit(solution)/shard_map/ppermute | solution.py:18
  96.6 16.8 %all-to-all-start = ((bf16[2,2,131072]{2,1,0:T(2,128)(2,1)}), bf16[2,2,131072]{2,1,0:T(2,128)(2,1)S(1)}, u32[]{:S(2)}, u32[]{:S(2)}) async-start(bf16[2,2,131072]{2,1,0:T(2,128)(2,1)} %reshape.320), calls=%async_computation | async-start | bytes 2097152 | tf_op jit(solution)/shard_map/all_to_all | solution.py:68
  100.2 193.3 %all-gather.5.cloned.1.call-start = ((), (), s32[]{:S(2)}) async-start(), calls=%async_computation.3 | async-start | bytes 10485760 | tf_op jit(solution)/shard_map/all_gather | solution.py:23
  102.3 2.1 collective-permute-start.1
  124.4 2.7 copy-start.15
  125.8 2.1 collective-permute-start
  127.5 0.8 copy-start.8
  127.5 0.8 copy-start.9
  127.5 0.8 copy-start.10
  127.5 0.8 copy-start.11
  127.5 0.8 copy-start.14
  130.2 1.4 copy-start
  131.1 0.7 copy-start.7
  132.6 6.4 %collective-permute-start.3 = (f32[4,1024,128]{2,1,0:T(8,128)S(1)}, f32[4,1024,128]{2,1,0:T(8,128)S(1)}, u32[]{:S(2)}, u32[]{:S(2)}) collective-permute-start(f32[4,1024,128]{2,1,0:T(8,128)S(1)} %convolution_add_fusion), channel_id=1, source_target_pairs={{0,1},{1,0},{2,3},{3,2},{4,5},{5,4},{6,7},{7,6},{8,9},{9,8},{10,11... | collective-permute-start | bytes 6291464 | tf_op jit(solution)/shard_map/ppermute | solution.py:18
  138.9 1.3 copy-start.2
  141.9 0.7 copy-start.17
  147.5 17.6 %copy-start.12 = (f32[1,128,64]{1,2,0:T(8,128)S(1)}, f32[1,128,64]{1,2,0:T(8,128)}, u32[]{:S(2)}) copy-start(f32[1,128,64]{1,2,0:T(8,128)} %get-tuple-element.150) | copy-start | bytes 98308
  147.5 17.6 %copy-start.13 = (f32[1,64,128]{2,1,0:T(8,128)S(1)}, f32[1,64,128]{2,1,0:T(8,128)}, u32[]{:S(2)}) copy-start(f32[1,64,128]{2,1,0:T(8,128)} %copy.62) | copy-start | bytes 98308
  293.5 8.8 %copy-start.4 = (f32[128,64]{0,1:T(8,128)S(1)}, f32[128,64]{0,1:T(8,128)}, u32[]{:S(2)}) copy-start(f32[128,64]{0,1:T(8,128)} %copy.65) | copy-start | bytes 98308
  302.3 1.6 copy-start.1
  302.3 1.6 copy-start.6
  303.9 2.7 copy-start.5
Sparse Core Ops, SparseCore 0:
  142.1 151.4 all-gather.4
where the time goes:
time: 317 us; the launch traced here: 315 us
  waiting for transfers between devices  142 us (45%)
  other arithmetic  74.1 us (23%)
  local copies, waits for them, and re-layouts  45.6 us (14%)
  starting transfers between devices  16.5 us (5%)
  blocking collectives  15.4 us (5%)
  between operations  13.9 us (4%)
  matrix products  8.22 us (3%)
    all_gather x1, waiting for transfers between devices, prefix_2(): everything = jax.tree.map(lambda part: lax.all_gather(part, axis), shard)  125 us
    unnamed x4, other arithmetic  57.9 us
    unnamed x46, local copies, waits for them, and re-layouts  22.8 us
    all_gather x1, blocking collectives, prefix_2(): everything = jax.tree.map(lambda part: lax.all_gather(part, axis), shard)  15.4 us
    all_to_all x3, local copies, waits for them, and re-layouts, on_device(): lax.all_to_all(x_raw, 'head', split_axis=2, concat_axis=1, tiled=True)  9.54 us
    all_to_all x1, waiting for transfers between devices, on_device(): lax.all_to_all(x_raw, 'head', split_axis=2, concat_axis=1, tiled=True)  8.91 us
    select_n x4, other arithmetic, hop(): return jax.tree.map(lambda a, b: jnp.where(reached, a, b), new, before)  8.64 us
  transfers between devices with their start and end apart: 8, of which 6 were waited for; matrix products, arithmetic and copies ran while one was open for 28% of the time, Pallas kernels for 0%

commit v1 on v0

--- a/solution.py
+++ b/solution.py
@@ -6,6 +6,13 @@
 STATE = 128
 SPAN = 128
 NORM_EPSILON = 1e-05
+
+
+def stacked_exchange(x, name, split, join):
+    devices = lax.axis_size(name)
+    shards = jnp.stack(jnp.split(x, devices, axis=split), axis=0)
+    shards = lax.all_to_all(shards, name, split_axis=0, concat_axis=0)
+    return jnp.concatenate(shards, axis=join)
 
 
 def shifted(value, axis, steps):
@@ -65,7 +72,7 @@
     norm_gain,
 ):
     x_ex, bc_ex, dt_ex = (
-        lax.all_to_all(x_raw, "head", split_axis=2, concat_axis=1, tiled=True),
+        stacked_exchange(x_raw, "head", 2, 1),
         lax.all_to_all(bc_raw, "head", split_axis=2, concat_axis=1, tiled=True),
         lax.all_to_all(dt_raw, "head", split_axis=2, concat_axis=1, tiled=True),
     )

time: 317 us -> 247 us (0.78)
  other arithmetic: 74.1 us -> 29.1 us
  local copies, waits for them, and re-layouts: 45.6 us -> 21.4 us
    unnamed x4 -> x3, other arithmetic: 57.9 us -> 12.5 us
    unnamed x46 -> x49, local copies, waits for them, and re-layouts: 22.8 us -> 8.67 us
    all_to_all x3 -> x0, local copies, waits for them, and re-layouts: 9.54 us -> none  [on_device(): lax.all_to_all(x_raw, 'head', split_axis=2, concat_axis=1, tiled=True)]
  transfers between devices with their start and end apart: 8 -> 8, of which waited for: 6 -> 6; matrix products, arithmetic and copies ran while one was open for 28% -> 13% of each run, Pallas kernels for 0% -> 0%
where the time goes in v1:
time: 247 us; the launch traced here: 246 us
  waiting for transfers between devices  141 us (57%)
  other arithmetic  29.1 us (12%)
  local copies, waits for them, and re-layouts  21.4 us (9%)
  starting transfers between devices  16.5 us (7%)
  blocking collectives  15.4 us (6%)
  between operations  13.8 us (6%)
  matrix products  8.2 us (3%)
    all_gather x1, waiting for transfers between devices, prefix_2(): everything = jax.tree.map(lambda part: lax.all_gather(part, axis), shard)  124 us
    all_gather x1, blocking collectives, prefix_2(): everything = jax.tree.map(lambda part: lax.all_gather(part, axis), shard)  15.4 us
    unnamed x3, other arithmetic  12.5 us
    all_to_all x1, waiting for transfers between devices, stacked_exchange(): shards = lax.all_to_all(shards, name, split_axis=0, concat_axis=0)  8.92 us
    unnamed x49, local copies, waits for them, and re-layouts  8.67 us
    select_n x4, other arithmetic, hop(): return jax.tree.map(lambda a, b: jnp.where(reached, a, b), new, before)  8.64 us
  transfers between devices with their start and end apart: 8, of which 6 were waited for; matrix products, arithmetic and copies ran while one was open for 13% of the time, Pallas kernels for 0%

profile of v1, /device:TPU:0, one launch (start us, length us, event | category | flops | bytes accessed | tf_op | source)
XLA Modules:
  0.0 246.0 jit_solution(8992217306841146224)
XLA Ops:
  6.5 0.9 copy.104
  7.4 0.6 broadcast.182
  8.0 0.9 reduce.5
  8.9 0.7 reshape.319
  9.6 4.2 %all-to-all-start.2 = ((bf16[2,2,2048]{2,1,0:T(2,128)(2,1)}), bf16[2,2,2048]{2,1,0:T(2,128)(2,1)S(1)}, u32[]{:S(2)}, u32[]{:S(2)}) async-start(bf16[2,2,2048]{2,1,0:T(2,128)(2,1)} %reshape.319), calls=%async_computation.2 | async-start | bytes 32768 | tf_op jit(solution)/shard_map/all_to_all | solution.py:77
  13.8 1.3 slice_bitcast_fusion.1
  15.1 0.7 fusion.27
  15.8 1.1 pad_maximum_fusion
  16.9 0.7 copy.98
  17.6 11.6 %reduce.6 = bf16[2048,64]{1,0:T(8,128)(2,1)S(1)} reduce(bf16[2048,1,64]{2,1,0:T(2,128)(2,1)S(1)} %bitcast.105, bf16[]{:T(256)} %broadcast.182), dimensions={1}, to_apply=%bitcast.85.reduce_sub_computation | reduce | bytes 524290
  29.2 1.1 reshape.321
  30.3 3.4 %all-to-all-start.1 = ((bf16[2,2,32768]{2,1,0:T(2,128)(2,1)}), bf16[2,2,32768]{2,1,0:T(2,128)(2,1)S(1)}, u32[]{:S(2)}, u32[]{:S(2)}) async-start(bf16[2,2,32768]{2,1,0:T(2,128)(2,1)} %reshape.321), calls=%async_computation.1 | async-start | bytes 524288 | tf_op jit(solution)/shard_map/all_to_all | solution.py:76
  33.8 0.1 reshape.320
  34.1 0.7 broadcast_multiply_fusion
  34.9 0.2 reduce_window_sum.13
  35.3 0.1 broadcast_in_dim.63
  35.4 4.0 %all-to-all-done.1 = bf16[2,2,32768]{2,1,0:T(2,128)(2,1)S(1)} async-done(((bf16[2,2,32768]{2,1,0:T(2,128)(2,1)}), bf16[2,2,32768]{2,1,0:T(2,128)(2,1)S(1)}, u32[]{:S(2)}, u32[]{:S(2)}) %all-to-all-start.1) | async-done | bytes 262176 | tf_op jit(solution)/shard_map/all_to_all | solution.py:76
  39.5 3.6 %all-to-all-start = ((bf16[2,1,64,4096]{3,2,1,0:T(8,128)(2,1)}), bf16[2,1,64,4096]{3,2,1,0:T(8,128)(2,1)S(1)}, u32[]{:S(2)}, u32[]{:S(2)}) async-start(bf16[2,1,64,4096]{3,2,1,0:T(8,128)(2,1)} %pad_maximum_fusion), calls=%async_computation | async-start | bytes 2097152 | tf_op jit(solution)/shard_map/all_to_all | solution.py:14
  43.2 0.7 copy.109
  43.9 0.4 reshape.322
  44.3 0.6 copy.99
  44.9 0.2 all_to_all.23
  45.2 1.3 collective-permute-start.1
  46.5 0.6 broadcast_select_fusion.1
  47.1 0.2 collective-permute-done.1
  47.4 8.9 %all-to-all-done = bf16[2,1,64,4096]{3,2,1,0:T(8,128)(2,1)S(1)} async-done(((bf16[2,1,64,4096]{3,2,1,0:T(8,128)(2,1)}), bf16[2,1,64,4096]{3,2,1,0:T(8,128)(2,1)S(1)}, u32[]{:S(2)}, u32[]{:S(2)}) %all-to-all-start) | async-done | bytes 1048608 | tf_op jit(solution)/shard_map/all_to_all | solution.py:14
  56.3 1.5 collective-permute-start
  57.8 0.3 multiply_convert_fusion.4
  58.2 0.2 copy.101
  58.5 0.3 maximum_convert_fusion
  58.8 0.1 copy-done.8
  59.0 1.3 multiply_convert_fusion.3
  60.3 0.5 copy.115
  60.8 0.9 broadcast_in_dim.66
  61.8 0.2 fusion.8
  62.0 0.2 copy-done
  62.2 0.3 copy-done.7
  62.5 0.8 convolution_add_fusion
  63.2 2.4 collective-permute-start.3
  65.6 3.8 %collective-permute-done.3 = f32[4,1024,128]{2,1,0:T(8,128)S(1)} collective-permute-done((f32[4,1024,128]{2,1,0:T(8,128)S(1)}, f32[4,1024,128]{2,1,0:T(8,128)S(1)}, u32[]{:S(2)}, u32[]{:S(2)}) %collective-permute-start.3) | collective-permute-done | bytes 2097184 | tf_op jit(solution)/shard_map/ppermute | solution.py:25
  69.4 1.3 copy-done.2
  70.8 1.7 select_add_fusion
  72.5 0.6 copy-done.19
  73.2 0.7 broadcast_in_dim.71
  73.9 0.8 broadcast_in_dim.72
  74.7 1.3 mul.290
  76.1 0.6 iota_compare_fusion
  76.7 0.7 copy.108
  77.4 0.7 copy.111
  78.1 15.4 %all-gather.2 = f32[4,4,1024]{2,1,0:T(4,128)S(1)} all-gather(f32[1,4,1024]{2,1,0:T(4,128)} %get-tuple-element.162), channel_id=2, replica_groups=mesh['groups'=2,'seq'=4,'head'=2,'sub'=2] {'seq'}, dimensions={0}, use_global_device_ids=true | all-gather | bytes 81920 | tf_op jit(solution)/shard_map/all_gather | solution.py:30
  93.5 0.9 fusion.22
  94.4 1.3 copy.97
  95.7 3.9 %fusion.1 = f32[4,16,64,128]{3,2,1,0:T(8,128)} fusion(bf16[128,4,16,64]{0,3,2,1:T(8,128)(2,1)} %bitcast.112, f32[4,16,128]{2,1,0:T(8,128)S(1)} %bitcast.122, f32[4,16,128]{2,1,0:T(8,128)S(1)} %bitcast.123, f32[4,128,128]{2,1,0:T(8,128)} %fusion.22, pred[128,128]{1,0:T(8,128)(4,1)} %iota_compare_fusion), kind=kOutput, calls=%fused_computation.4 | convolution fusion | flops 139460608 | bytes 3489792 | tf_op jit(solution)/shard_map/bgjts,bsgjp->btgjp/dot_general | solution.py:123
  99.6 124.5 %all-gather.5.cloned.1.call-done = f32[16,1024,128]{2,1,0:T(8,128)} async-done(((f32[4,1024,128]{2,1,0:T(8,128)}), f32[16,1024,128]{2,1,0:T(8,128)}) %all-gather.5.cloned.1.call-update) | async-done | bytes 8388624 | tf_op jit(solution)/shard_map/all_gather | solution.py:30
  224.1 8.8 %while.9 = (s32[]{:T(128)}, f32[4,1024,128]{2,1,0:T(8,128)S(1)}, s32[]{:T(128)}, f32[4,4,1024]{2,1,0:T(4,128)S(1)}, f32[4,4,1024,128]{3,2,1,0:T(8,128)}, /*index=5*/s32[]{:T(128)}, s32[]{:T(128)}) while((s32[]{:T(128)}, f32[4,1024,128]{2,1,0:T(8,128)S(1)}, s32[]{:T(128)}, f32[4,4,1024]{2,1,0:T(4,128)S(1)}, ...), condition=%wide.region_2.3_spmd.clone, body=%wide.region_1.2_spmd.clone.sunk | while | flops 2097156 | bytes 6340713 | solution.py:42
  224.1 2.2 fusion.32
  226.3 2.2 fusion.32
  228.5 2.2 fusion.32
  230.7 2.2 fusion.32
  232.9 0.1 broadcast_in_dim.68
  233.0 1.4 copy-done.1
  234.5 2.6 %multiply_reduce_fusion = (f32[128,4]{0,1:T(4,128)S(1)}, f32[1,128,4,1024]{1,3,2,0:T(8,128)S(1)}) fusion(f32[1,128,4,1024]{1,3,2,0:T(8,128)S(1)} %bitcast.98, f32[4,1024]{1,0:T(4,128)S(1)} %broadcast_in_dim.72, f32[1,128,4,1024]{1,3,2,0:T(8,128)S(1)} %bitcast.101, bf16[1,128,4,2,128]{1,4,3,2,0:T(8,128)(2,1)S(1)} %bitcast.109, ...), kind=kOutput, calls=%fused_computation.19 | convolution fusion | flops 139460096 | bytes 12748801 | tf_op jit(solution)/shard_map/btgn,bgqn->btgq/dot_general | solution.py:158
  237.1 0.7 multiply_convert_fusion.2
  237.9 1.3 copy.113
  (63 shorter events, 1.1 us)
Async XLA Ops:
  6.5 8.6 %copy-start.12 = (f32[4,4096]{1,0:T(4,128)S(1)}, f32[4,4096]{1,0:T(4,128)}, u32[]{:S(2)}) copy-start(f32[4,4096]{1,0:T(4,128)} %param.16) | copy-start | bytes 196612
  6.5 9.3 %copy-start.16 = (f32[4,1024]{1,0:T(4,128)S(1)}, f32[4,1024]{1,0:T(4,128)}, u32[]{:S(2)}) copy-start(f32[4,1024]{1,0:T(4,128)} %param.18) | copy-start | bytes 49156
  9.6 20.8 %all-to-all-start.2 = ((bf16[2,2,2048]{2,1,0:T(2,128)(2,1)}), bf16[2,2,2048]{2,1,0:T(2,128)(2,1)S(1)}, u32[]{:S(2)}, u32[]{:S(2)}) async-start(bf16[2,2,2048]{2,1,0:T(2,128)(2,1)} %reshape.319), calls=%async_computation.2 | async-start | bytes 32768 | tf_op jit(solution)/shard_map/all_to_all | solution.py:77
  13.8 3.1 %copy-start.20 = (f32[64]{0:T(128)S(1)}, f32[64]{0:T(128)}, u32[]{:S(2)}) copy-start(f32[64]{0:T(128)} %param.21) | copy-start | bytes 772
  13.8 3.1 %copy-start.3 = (bf16[1,64,2048]{2,1,0:T(8,128)(2,1)S(1)}, bf16[1,64,2048]{2,1,0:T(8,128)(2,1)}, u32[]{:S(2)}) copy-start(bf16[1,64,2048]{2,1,0:T(8,128)(2,1)} %param.14) | copy-start | bytes 786436
  16.9 17.3 %copy-start.18 = (f32[64]{0:T(128)S(1)}, f32[64]{0:T(128)}, u32[]{:S(2)}) copy-start(f32[64]{0:T(128)} %param.20) | copy-start | bytes 772
  30.3 9.1 %all-to-all-start.1 = ((bf16[2,2,32768]{2,1,0:T(2,128)(2,1)}), bf16[2,2,32768]{2,1,0:T(2,128)(2,1)S(1)}, u32[]{:S(2)}, u32[]{:S(2)}) async-start(bf16[2,2,32768]{2,1,0:T(2,128)(2,1)} %reshape.321), calls=%async_computation.1 | async-start | bytes 524288 | tf_op jit(solution)/shard_map/all_to_all | solution.py:76
  35.4 11.1 %collective-permute-start.2 = (f32[4,1024]{1,0:T(4,128)S(1)}, f32[4,1024]{1,0:T(4,128)S(1)}, u32[]{:S(2)}, u32[]{:S(2)}) collective-permute-start(f32[4,1024]{1,0:T(4,128)S(1)} %broadcast_in_dim.63), channel_id=1, source_target_pairs={{0,1},{1,0},{2,3},{3,2},{4,5},{5,4},{6,7},{7,6},{8,9},{9,8},{10,11... | collective-permute-start | bytes 49160 | tf_op jit(solution)/shard_map/ppermute | solution.py:25
  39.5 16.8 %all-to-all-start = ((bf16[2,1,64,4096]{3,2,1,0:T(8,128)(2,1)}), bf16[2,1,64,4096]{3,2,1,0:T(8,128)(2,1)S(1)}, u32[]{:S(2)}, u32[]{:S(2)}) async-start(bf16[2,1,64,4096]{3,2,1,0:T(8,128)(2,1)} %pad_maximum_fusion), calls=%async_computation | async-start | bytes 2097152 | tf_op jit(solution)/shard_map/all_to_all | solution.py:14
  43.1 181.0 %all-gather.5.cloned.1.call-start = ((), (), s32[]{:S(2)}) async-start(), calls=%async_computation.3 | async-start | bytes 10485760 | tf_op jit(solution)/shard_map/all_gather | solution.py:30
  43.9 13.9 %copy-start.17 = (f32[1024]{0:T(1024)S(1)}, f32[1024]{0:T(1024)}, u32[]{:S(2)}) copy-start(f32[1024]{0:T(1024)} %param.19) | copy-start | bytes 12292
  45.2 2.1 collective-permute-start.1
  56.3 2.1 collective-permute-start
  58.2 0.7 copy-start.8
  58.2 0.7 copy-start.9
  58.2 0.7 copy-start.10
  58.2 0.7 copy-start.11
  58.2 0.7 copy-start.15
  60.8 1.4 copy-start
  61.8 0.7 copy-start.7
  63.2 6.2 %collective-permute-start.3 = (f32[4,1024,128]{2,1,0:T(8,128)S(1)}, f32[4,1024,128]{2,1,0:T(8,128)S(1)}, u32[]{:S(2)}, u32[]{:S(2)}) collective-permute-start(f32[4,1024,128]{2,1,0:T(8,128)S(1)} %convolution_add_fusion), channel_id=1, source_target_pairs={{0,1},{1,0},{2,3},{3,2},{4,5},{5,4},{6,7},{7,6},{8,9},{9,8},{10,11... | collective-permute-start | bytes 6291464 | tf_op jit(solution)/shard_map/ppermute | solution.py:25
  69.4 1.3 copy-start.2
  72.5 0.7 copy-start.19
  78.1 17.6 %copy-start.13 = (f32[1,128,64]{1,2,0:T(8,128)S(1)}, f32[1,128,64]{1,2,0:T(8,128)}, u32[]{:S(2)}) copy-start(f32[1,128,64]{1,2,0:T(8,128)} %get-tuple-element.150) | copy-start | bytes 98308
  78.1 17.6 %copy-start.14 = (f32[1,64,128]{2,1,0:T(8,128)S(1)}, f32[1,64,128]{2,1,0:T(8,128)}, u32[]{:S(2)}) copy-start(f32[1,64,128]{2,1,0:T(8,128)} %copy.108) | copy-start | bytes 98308
  224.1 8.8 %copy-start.4 = (f32[128,64]{0,1:T(8,128)S(1)}, f32[128,64]{0,1:T(8,128)}, u32[]{:S(2)}) copy-start(f32[128,64]{0,1:T(8,128)} %copy.111) | copy-start | bytes 98308
  232.9 1.6 copy-start.1
  232.9 1.6 copy-start.6
  234.5 2.7 %copy-start.5 = (f32[4,1024]{1,0:T(4,128)S(1)}, f32[4,1024]{1,0:T(4,128)}, u32[]{:S(2)}) copy-start(f32[4,1024]{1,0:T(4,128)} %mul.290) | copy-start | bytes 49156
Sparse Core Ops, SparseCore 0:
  72.6 151.4 all-gather.4
